TPU v7x, 128 devices: a whole 4x4x4 slice. The times are simulated.
128 devices in a mesh: tm: 16 (over z, x), tile: 8 (over y, core).
Axes of the slice: x: 4, y: 4, z: 4, core: 2. Of those that a mesh axis runs over, the one named last changes fastest.
Arguments:
- frames: bfloat16 [64, 64, 64, 128], P('tm', 'tile'), may hold values from -6 to 6
- cotangent: bfloat16 [64, 64, 64, 128], P('tm', 'tile'), may hold values from -6 to 6
- w_in: bfloat16 [3, 3, 128, 128], replicated, may hold values from -0.1875 to 0.1875
- w_out: bfloat16 [3, 3, 128, 128], replicated, may hold values from -0.1875 to 0.1875
- skip: float32 [128], replicated, may hold values from 0.5 to 1.5
- log_decay: float32 [64, 128], P('tm'), may hold values from -1 to 0
Outputs:
- output: bfloat16 [64, 64, 64, 128], P('tm', 'tile')
- grad_frames: bfloat16 [64, 64, 64, 128], P('tm', 'tile')
- grad_w_in: float32 [3, 3, 128, 128], replicated
- grad_w_out: float32 [3, 3, 128, 128], replicated
All inputs are finite; a program needn't handle non-finite values.
Results may differ from a plain program's by a relative error of at most 0.0029.
Values may be sent and summed in bfloat16 or wider, within the bound.
A program may use at most 64 MiB of HBM per device.

v0:
```python
import functools
import math

import jax
import jax.numpy as jnp
from jax import lax
from jax.experimental import pallas as pl
from jax.experimental.pallas import tpu as pltpu
from jax.sharding import PartitionSpec as P

MESH = pl.DeviceIdType.MESH
F32 = jnp.float32
BF16 = jnp.bfloat16
ROOT = 5


def encode(v):
    square = v * v
    return (v * (square * square)).astype(BF16)


def decode(code):
    w = code.astype(F32)
    root = jnp.exp2(jnp.log2(jnp.abs(w)) * (1.0 / ROOT))
    return jnp.where(w < 0.0, -root, root)


def chain_kernel(
    dims,
    frames, cot, w_in, w_out, skip, log_decay,
    own_out, mate_out, sums,
    X, Y, S, X3, Y3, S3, ST,
    WA, WB, COEF, DG,
    DR, LS, FIN, RF, EF, INC,
    G, GC, R1, R3, MO,
    load_sem, in_send, in_recv, halo_send, halo_recv,
    carry_send, carry_recv, fin_send, back_send, inc_recv, ar_send, ar_recv, mo_send, mo_recv,
):
    nt, nx, ny, factor = dims
    T, R, W, CH = frames.shape
    RC = 2 * R
    n = nx
    pos = RC * W
    half = 9 * CH
    group = half // 3
    chunk = group // (n * n)

    tm = lax.axis_index("tm")
    tile = lax.axis_index("tile")
    ntile = ny * 2
    z, x = lax.div(tm, nx), lax.rem(tm, nx)
    y, core = lax.div(tile, 2), lax.rem(tile, 2)
    forward = core == 1
    mate = (tm, y * 2 + 1 - core)

    def on_tm(d):
        return (lax.rem(tm + d, nt), tile)

    where_on = {"x": x, "y": y, "z": z}

    def axis_peer(axis, d):
        if axis == "x":
            return (z * nx + lax.rem(x + d, nx), tile)
        if axis == "z":
            return (lax.rem(z + d, nt // nx) * nx + x, tile)
        return (tm, lax.rem(y + d, ny) * 2 + core)

    def remote(src, dst, send, recv, device):
        return pltpu.make_async_remote_copy(
            src, dst, send, recv, device_id=device, device_id_type=MESH
        )

    def took(ref, sem):
        pltpu.make_async_copy(ref, ref, sem).wait()

    barrier = pltpu.get_barrier_semaphore()
    for d in range(1, nt):
        pl.semaphore_signal(barrier, inc=1, device_id=on_tm(d), device_id_type=MESH)
    for d in range(1, ntile):
        pl.semaphore_signal(
            barrier, inc=1, device_id=(tm, lax.rem(tile + d, ntile)), device_id_type=MESH
        )

    own_rows = pl.ds(1 + core * R, R)

    def load(first, second):
        pltpu.make_async_copy(first, X.at[:, own_rows], load_sem.at[0]).start()
        pltpu.make_async_copy(second, Y.at[:, own_rows], load_sem.at[1]).start()

    @pl.when(forward)
    def _():
        load(frames, cot)

    @pl.when(core == 0)
    def _():
        load(cot, frames)

    @pl.when(y == 0)
    def _():
        for field in (X, Y, S):
            field[:, 0] = jnp.zeros((T, W, CH), BF16)

    @pl.when(y == ny - 1)
    def _():
        for field in (X, Y, S):
            field[:, RC + 1] = jnp.zeros((T, W, CH), BF16)

    dec = jnp.exp(log_decay[...])
    whole = dec[0:1]
    for t in range(1, T):
        whole = whole * dec[t : t + 1]
    DG[tm] = jnp.broadcast_to(whole, (8, CH))
    one = jnp.ones((1, CH), F32)
    reach = None
    for i in range(T):
        a = jnp.where(forward, dec[i : i + 1], one if i == 0 else dec[T - i : T - i + 1])
        b = jnp.where(forward, 1.0 - dec[i : i + 1], one)
        c = jnp.where(forward, one, 1.0 - dec[T - 1 - i : T - i])
        reach = a if reach is None else reach * a
        COEF[i : i + 1] = a
        COEF[T + i : T + i + 1] = b
        COEF[2 * T + i : 2 * T + i + 1] = c
        COEF[3 * T + i : 3 * T + i + 1] = c * reach
    last = jnp.where(forward, one, dec[0:1])

    def weights(dst, plain, turned):
        @pl.when(forward)
        def _():
            dst[...] = plain[...]

        @pl.when(core == 0)
        def _():
            for k in range(9):
                dst[k * CH : (k + 1) * CH, :] = turned[(8 - k) * CH : (9 - k) * CH, :].T

    weights(WA, w_in, w_out)

    pl.semaphore_wait(barrier, nt - 1 + ntile - 1)

    def send_inputs(first, second):
        remote(first, X.at[:, own_rows], in_send.at[0], in_recv.at[0], mate).start()
        edge(0)
        remote(second, Y.at[:, own_rows], in_send.at[1], in_recv.at[1], mate).start()
        edge(1)

    edge_src = pl.ds(core * (R - 1), 1)
    edge_dst = pl.ds((1 - core) * (RC + 1), 1)
    next_y = y + 2 * core - 1
    has_next = (next_y >= 0) & (next_y < ny)
    safe_y = lax.min(lax.max(next_y, 0), ny - 1)

    def edge_copies(which):
        copies = []
        for c in range(2):
            src = (frames, cot)[(c == 1) == (which == 1)]
            dst = (X, Y)[which]
            copies.append(
                remote(
                    src.at[:, edge_src], dst.at[:, edge_dst],
                    halo_send.at[which, c], halo_recv.at[which, 1 - core],
                    (tm, safe_y * 2 + c),
                )
            )
        return copies

    def edge(which):
        @pl.when(has_next)
        def _():
            for copy in edge_copies(which):
                copy.start()

    @pl.when(forward)
    def _():
        send_inputs(cot, frames)

    @pl.when(core == 0)
    def _():
        send_inputs(frames, cot)

    for d in range(1, nt):
        remote(DG.at[tm], DG.at[tm], carry_send.at[0], carry_recv.at[0], on_tm(d)).start()

    def edge_took(which, field):
        @pl.when(y > 0)
        def _():
            took(field.at[:, pl.ds(0, 1)], halo_recv.at[which, 0])

        @pl.when(y < ny - 1)
        def _():
            took(field.at[:, pl.ds(RC + 1, 1)], halo_recv.at[which, 1])

    col = lax.broadcasted_iota(jnp.int32, (1, W, CH), 1)

    def widen(src, dst, row0, count):
        def step(k, _):
            r = row0 + k
            for t in range(T):
                v = src[t, pl.ds(r, 1)].astype(F32)
                left = jnp.where(col == 0, 0.0, pltpu.roll(v, 1, 1))
                right = jnp.where(col == W - 1, 0.0, pltpu.roll(v, W - 1, 1))
                dst[t, pl.ds(r, 1), :, 0:CH] = left.astype(BF16)
                dst[t, pl.ds(r, 1), :, CH : 2 * CH] = src[t, pl.ds(r, 1)]
                dst[t, pl.ds(r, 1), :, 2 * CH : 3 * CH] = right.astype(BF16)
            return 0

        lax.fori_loop(0, count, step, 0)

    def conv(src3, t, row0, count, weight):
        taps = jnp.concatenate(
            [src3[t, pl.ds(row0 + i, count)].reshape(count * W, 3 * CH) for i in range(3)], axis=-1
        )
        return jnp.dot(taps, weight[...], preferred_element_type=F32)

    def frame_of(i):
        return core * i + (1 - core) * (T - 1 - i)

    def local_scan(*spans):
        spans = [span for span in spans if span[1]]
        if not spans:
            return
        taps = jnp.concatenate(
            [
                jnp.concatenate([X3[:, pl.ds(row0 + i, count)] for row0, count in spans], axis=1)
                .reshape(-1, 3 * CH)
                for i in range(3)
            ],
            axis=-1,
        )
        drive = jnp.dot(taps, WA[...], preferred_element_type=F32)
        per_frame = drive.shape[0] // T
        for t in range(T):
            at = t * per_frame
            for row0, count in spans:
                rows = pl.ds(pl.multiple_of(row0 * W, W), count * W)
                DR[t, rows, :] = drive[at : at + count * W]
                at += count * W
        for row0, count in spans:
            rows = pl.ds(pl.multiple_of(row0 * W, W), count * W)
            for i in range(T):
                value = COEF[T + i : T + i + 1] * DR[frame_of(i), rows, :]
                if i:
                    value = value + COEF[i : i + 1] * LS[i - 1, rows, :]
                LS[i, rows, :] = value
            FIN[rows, :] = encode(last * value)
            send_finals(row0, count)

    def rows_of(ref, k):
        return ref.at[pl.ds(pl.multiple_of(k * W, W), W)]

    def send_finals(row0, count):
        for r in range(count):
            k = row0 + lax.rem(r + tm, count)

            @pl.when(k != tm)
            def _():
                remote(
                    rows_of(FIN, k), RF.at[tm], fin_send.at[k], carry_recv.at[1], (k, tile)
                ).start()

    took(X.at[:, pl.ds(1, R)], load_sem.at[0])
    widen(X, X3, 1 + core * R, R)
    local_scan((core * R + 1, R - 2))
    took(X.at[:, pl.ds(1, R)], in_recv.at[0])
    widen(X, X3, 1 + (1 - core) * R, R)
    if R > 2:
        local_scan(((1 - core) * (R - 1) + core, R))
    else:
        local_scan((1, RC - 2))
    edge_took(0, X)
    widen(X, X3, 0, 1)
    widen(X, X3, RC + 1, 1)
    local_scan((0, 1), (RC - 1, 1))

    others = pl.ds(0, nt - 1)
    RF[tm] = FIN[pl.ds(pl.multiple_of(tm * W, W), W), :]

    weights(WB, w_out, w_in)
    took(Y.at[:, pl.ds(1, R)], load_sem.at[1])
    took(Y.at[:, pl.ds(1, R)], in_recv.at[1])
    edge_took(1, Y)
    widen(Y, Y3, 0, RC + 2)

    took(DG.at[others], carry_recv.at[0])
    took(RF.at[others], carry_recv.at[1])
    carry = jnp.zeros((W, CH), F32)
    for i in range(nt):
        k = core * i + (1 - core) * (nt - 1 - i)
        EF[k] = encode(carry)

        @pl.when(k != tm)
        def _():
            remote(EF.at[k], rows_of(INC, tm), back_send.at[k], inc_recv.at[tm], (k, tile)).start()

        if i < nt - 1:
            carry = DG[k, 0:1, :] * carry + decode(RF[k])
    INC[pl.ds(pl.multiple_of(tm * W, W), W), :] = EF[tm]

    def finish(row0, count):
        for k in range(row0, row0 + count):

            @pl.when(tm != k)
            def _():
                took(rows_of(INC, k), inc_recv.at[k])

        rows = slice(row0 * W, (row0 + count) * W)
        incoming = decode(INC[rows, :])
        for i in range(T):
            value = (
                COEF[2 * T + i : 2 * T + i + 1] * LS[i, rows, :]
                + COEF[3 * T + i : 3 * T + i + 1] * incoming
            )
            S[frame_of(i), 1 + row0 : 1 + row0 + count] = value.astype(BF16).reshape(count, W, CH)

    finish(1, RC - 2)
    finish(0, 1)
    finish(RC - 1, 1)

    up = remote(
        S.at[:, pl.ds(1, 1)], S.at[:, pl.ds(RC + 1, 1)], halo_send.at[2, 0], halo_recv.at[2, 1],
        (tm, lax.max(y - 1, 0) * 2 + core),
    )
    down = remote(
        S.at[:, pl.ds(RC, 1)], S.at[:, pl.ds(0, 1)], halo_send.at[2, 1], halo_recv.at[2, 0],
        (tm, lax.min(y + 1, ny - 1) * 2 + core),
    )

    @pl.when(y > 0)
    def _():
        up.start()

    @pl.when(y < ny - 1)
    def _():
        down.start()

    orders = (("x", "y", "z"), ("y", "z", "x"), ("z", "x", "y"))
    steps = [(da, db) for da in range(n) for db in range(n) if da or db]
    steps.sort(key=lambda s: -sum(min(d, n - d) for d in s))

    def place(g, da, db):
        a, b = orders[g][:2]
        return lax.rem(where_on[a] + da, n) * n + lax.rem(where_on[b] + db, n)

    def plane_peer(g, da, db):
        at = dict(where_on)
        for axis, d in zip(orders[g], (da, db)):
            at[axis] = lax.rem(at[axis] + d, n)
        return (at["z"] * nx + at["x"], at["y"] * 2 + core)

    for t in range(T):
        ST[t] = S[t, 1 : RC + 1].reshape(pos, CH).T
    for g in range(3):
        first = core * (2 - g) + (1 - core) * g
        total = jnp.zeros((CH, 3 * CH), F32)
        for t in range(T):
            other = Y3[t, pl.ds(first, RC)].reshape(pos, 3 * CH)
            total = total + jnp.dot(ST[t], other, preferred_element_type=F32)
        total = total * factor

        @pl.when(forward)
        def _():
            for j in range(3):
                block = total[:, (2 - j) * CH : (3 - j) * CH]
                G[(g * 3 + j) * CH : (g * 3 + j + 1) * CH, :] = block
                GC[(g * 3 + j) * CH : (g * 3 + j + 1) * CH, :] = encode(block)

        @pl.when(core == 0)
        def _():
            for j in range(3):
                block = total[:, j * CH : (j + 1) * CH].T
                G[(g * 3 + j) * CH : (g * 3 + j + 1) * CH, :] = block
                GC[(g * 3 + j) * CH : (g * 3 + j + 1) * CH, :] = encode(block)

        for slot, (da, db) in enumerate(steps):
            q = place(g, da, db)
            remote(
                GC.at[pl.ds(pl.multiple_of(g * group + q * chunk, chunk), chunk)],
                R1.at[g, slot], ar_send.at[0], ar_recv.at[g], plane_peer(g, da, db),
            ).start()

    def conv_out(t):
        for side, (start, stage) in enumerate(((core * R, own_out), ((1 - core) * R, MO))):
            rows = pl.ds(start + 1, R)
            direct = skip[...] * X[t, rows].reshape(R * W, CH).astype(F32)
            value = conv(S3, t, start, R, WB) + direct
            stage[t] = value.astype(BF16).reshape(R, W, CH)
        remote(MO.at[t], mate_out.at[t], mo_send.at[t], mo_recv.at[t], mate).start()

    widen(S, S3, 1, RC)

    @pl.when(y > 0)
    def _():
        took(S.at[:, pl.ds(0, 1)], halo_recv.at[2, 0])

    @pl.when(y < ny - 1)
    def _():
        took(S.at[:, pl.ds(0, 1)], halo_recv.at[2, 1])

    widen(S, S3, 0, 1)
    widen(S, S3, RC + 1, 1)

    conv_out(0)
    conv_out(1)
    for g in range(3):
        took(R1.at[g], ar_recv.at[g])
        value = G[pl.ds(pl.multiple_of(g * group + place(g, 0, 0) * chunk, chunk), chunk), :]
        for slot in range(n * n - 1):
            value = value + decode(R1[g, slot])
        c = orders[g][2]
        r = where_on[c]
        R3[g, r] = value
        for d in range(1, n):
            remote(
                R3.at[g, r], R3.at[g, r], ar_send.at[1], ar_recv.at[3 + g], axis_peer(c, d)
            ).start()
    conv_out(2)
    base = core * half
    for g in range(3):
        took(R3.at[g, pl.ds(0, n - 1)], ar_recv.at[3 + g])
        value = R3[g, 0]
        for k in range(1, n):
            value = value + R3[g, k]
        rows = pl.ds(pl.multiple_of(base + g * group + place(g, 0, 0) * chunk, chunk), chunk)
        sums[rows, :] = value.astype(BF16)
        for da, db in steps:
            remote(
                sums.at[rows], sums.at[rows], ar_send.at[2], ar_recv.at[6 + g],
                plane_peer(g, da, db),
            ).start()
    conv_out(3)
    to_mate = []
    for g in range(3):
        rows = pl.ds(pl.multiple_of(base + g * group, group), group)
        took(sums.at[pl.ds(0, group - chunk)], ar_recv.at[6 + g])
        to_mate.append(
            remote(sums.at[rows], sums.at[rows], ar_send.at[3 + g], ar_recv.at[9 + g], mate)
        )
        to_mate[-1].start()

    for t in range(T):
        took(MO.at[t], mo_recv.at[t])
    for copy in to_mate:
        copy.wait_recv()

    for copy in to_mate:
        copy.wait_send()
    for t in range(T):
        took(MO.at[t], mo_send.at[t])
    took(R1, ar_send.at[0])
    took(R3.at[:, pl.ds(0, n - 1)], ar_send.at[1])
    took(sums.at[pl.ds(0, half - 3 * chunk)], ar_send.at[2])
    took(DG.at[others], carry_send.at[0])
    for k in range(nt):

        @pl.when(tm != k)
        def _():
            took(EF.at[0], fin_send.at[k])
            took(EF.at[0], back_send.at[k])

    for k in range(2):
        took(X.at[:, pl.ds(1, R)], in_send.at[k])

    @pl.when(has_next)
    def _():
        for which in range(2):
            for copy in edge_copies(which):
                copy.wait_send()

    @pl.when(y > 0)
    def _():
        up.wait_send()

    @pl.when(y < ny - 1)
    def _():
        down.wait_send()


def store_kernel(own_out, mate_out, sums, output, grad_frames, grad_in, grad_out, wide, sem):
    forward = lax.rem(lax.axis_index("tile"), 2) == 1
    half = grad_in.shape[0]

    def put(first, second):
        pltpu.make_async_copy(own_out, first, sem.at[0]).start()
        pltpu.make_async_copy(mate_out, second, sem.at[1]).start()

    @pl.when(forward)
    def _():
        put(output, grad_frames)

    @pl.when(jnp.logical_not(forward))
    def _():
        put(grad_frames, output)

    copies = []
    for k, dst in enumerate((grad_in, grad_out)):
        wide[k] = sums[k * half : (k + 1) * half, :].astype(F32)
        copies.append(pltpu.make_async_copy(wide.at[k], dst, sem.at[2 + k]))
        copies[-1].start()
    pltpu.make_async_copy(own_out, output, sem.at[0]).wait()
    pltpu.make_async_copy(mate_out, grad_frames, sem.at[1]).wait()
    for copy in copies:
        copy.wait()


def solution(mesh):
    nt, ntile = mesh.shape["tm"], mesh.shape["tile"]
    nx = math.isqrt(nt)
    ny = ntile // 2

    def step(frames, cot, w_in, w_out, skip, log_decay):
        T, R, W, CH = frames.shape
        factor = 1.0 / math.sqrt(T * nt * R * ntile * W)
        RC = 2 * R
        pos = RC * W
        n = nx
        half = 9 * CH
        chunk = half // 3 // (n * n)
        vm = pltpu.VMEM
        field = vm((T, RC + 2, W, CH), BF16)
        field3 = vm((T, RC + 2, W, 3 * CH), BF16)
        dma = pltpu.SemaphoreType.DMA
        hbm = pl.BlockSpec(memory_space=pl.ANY)
        vmem = pl.BlockSpec(memory_space=pltpu.VMEM)
        own_out, mate_out, sums = pl.pallas_call(
            functools.partial(chain_kernel, (nt, nx, ny, factor)),
            out_shape=(
                vm(frames.shape, BF16),
                vm(frames.shape, BF16),
                vm((2 * half, CH), BF16),
            ),
            in_specs=[hbm, hbm, vmem, vmem, vmem, vmem],
            out_specs=[vmem] * 3,
            scratch_shapes=[
                field, field, field, field3, field3, field3, vm((T, CH, pos), BF16),
                vm((half, CH), BF16), vm((half, CH), BF16), vm((4 * T, CH), F32), vm((nt, 8, CH), F32),
                vm((T, pos, CH), F32), vm((T, pos, CH), F32), vm((pos, CH), BF16),
                vm((nt, W, CH), BF16), vm((nt, W, CH), BF16), vm((pos, CH), BF16),
                vm((half, CH), F32), vm((half, CH), BF16),
                vm((3, n * n - 1, chunk, CH), BF16), vm((3, n, chunk, CH), F32), vm(frames.shape, BF16),
                dma((2,)), dma((2,)), dma((2,)), dma((3, 2)), dma((3, 2)),
                dma((1,)), dma((2,)), dma((nt,)), dma((nt,)), dma((nt,)),
                dma((6,)), dma((12,)), dma((T,)), dma((T,)),
            ],
            compiler_params=pltpu.CompilerParams(
                collective_id=0, has_side_effects=True, vmem_limit_bytes=65_300_000
            ),
        )(
            frames, cot, w_in.reshape(half, CH), w_out.reshape(half, CH),
            skip.reshape(1, CH), log_decay,
        )
        res = pl.pallas_call(
            store_kernel,
            out_shape=(
                jax.ShapeDtypeStruct(frames.shape, BF16),
                jax.ShapeDtypeStruct(frames.shape, BF16),
                jax.ShapeDtypeStruct((half, CH), F32),
                jax.ShapeDtypeStruct((half, CH), F32),
            ),
            in_specs=[vmem] * 3,
            out_specs=[hbm] * 4,
            scratch_shapes=[vm((2, half, CH), F32), dma((4,))],
            compiler_params=pltpu.CompilerParams(vmem_limit_bytes=8 * 2**20),
        )(own_out, mate_out, sums)
        return (res[0], res[1], res[2].reshape(3, 3, CH, CH), res[3].reshape(3, 3, CH, CH))

    block = P("tm", "tile", None, None)
    return jax.shard_map(
        step,
        mesh=mesh,
        in_specs=(block, block, P(), P(), P(), P("tm", None)),
        out_specs=(block, block, P(), P()),
        check_vma=False,
    )
```

profile of v0, /device:TPU:1, one launch (start us, length us, event | category | flops | bytes accessed | tf_op | source)
XLA Modules:
  0.0 47.3 jit_solution(17221438303709407345)
XLA Ops:
  0.6 45.2 %shard_map.93 = (bf16[4,8,64,128]{3,2,1,0:T(8,128)(2,1)S(1)}, bf16[4,8,64,128]{3,2,1,0:T(8,128)(2,1)S(1)}, bf16[2304,128]{1,0:T(8,128)(2,1)S(1)}) custom-call(bf16[4,8,64,128]{3,2,1,0:T(8,128)(2,1)} %frames.1, bf16[4,8,64,128]{3,2,1,0:T(8,128)(2,1)} %cot.1, bf16[1152,128]{1,0:T(8,128)(2,1)} %bitcast.5, bf16[1152,128]{1,0:T(8,128)(2,1)} %bitcast.6, ...), custom_call_target="tpu_custom_call" | custom-call | tf_op jit(solution)/shard_map/pallas_call | solution.py:523
  45.9 1.4 %shard_map.94 = (bf16[4,8,64,128]{3,2,1,0:T(8,128)(2,1)}, bf16[4,8,64,128]{3,2,1,0:T(8,128)(2,1)}, f32[1152,128]{1,0:T(8,128)}, f32[1152,128]{1,0:T(8,128)}) custom-call(bf16[4,8,64,128]{3,2,1,0:T(8,128)(2,1)S(1)} %get-tuple-element.11.own_out, bf16[4,8,64,128]{3,2,1,0:T(8,128)(2,1)S(1)} %get-tuple-element.12.mate_out, ...), custom_call_target="tpu_custom_call" | custom-call | tf_op jit(solution)/shard_map/pallas_call | solution.py:550
where the time goes:
time: 47.4 us; the launch traced here: 47.3 us
  Pallas kernels  46.6 us (98%)
  between operations  0.64 us (1%)
    pallas_call x1, Pallas kernels, step(): pl.pallas_call(functools.partial(chain_kernel, (nt, nx, ny, factor)), out...  45.2 us
    pallas_call x1, Pallas kernels, step(): pl.pallas_call(store_kernel, out_shape=(jax.ShapeDtypeStruct(frames.shape...  1.4 us

commit v1 on v0

--- a/solution.py
+++ b/solution.py
@@ -34,7 +34,7 @@
     DR, LS, FIN, RF, EF, INC,
     G, GC, R1, R3, MO,
     load_sem, in_send, in_recv, halo_send, halo_recv,
-    carry_send, carry_recv, fin_send, back_send, inc_recv, ar_send, ar_recv, mo_send, mo_recv,
+    carry_send, carry_recv, fin_send, back_send, inc_recv, ar_send, ar_recv, mo_send, mo_recv, round_sem,
 ):
     nt, nx, ny, factor = dims
     T, R, W, CH = frames.shape
@@ -73,13 +73,18 @@
     def took(ref, sem):
         pltpu.make_async_copy(ref, ref, sem).wait()
 
+    near = [axis_peer(axis, d) for axis in ("x", "y", "z") for d in (1, n - 1)]
+    across = [(tm, lax.rem(y + d, ny) * 2 + 1 - core) for d in (1, ny - 1)]
     barrier = pltpu.get_barrier_semaphore()
-    for d in range(1, nt):
-        pl.semaphore_signal(barrier, inc=1, device_id=on_tm(d), device_id_type=MESH)
-    for d in range(1, ntile):
-        pl.semaphore_signal(
-            barrier, inc=1, device_id=(tm, lax.rem(tile + d, ntile)), device_id_type=MESH
-        )
+    for device in [mate, *near, *across]:
+        pl.semaphore_signal(barrier, inc=1, device_id=device, device_id_type=MESH)
+
+    def greet(k):
+        for device in near:
+            pl.semaphore_signal(round_sem.at[k], inc=1, device_id=device, device_id_type=MESH)
+
+    def greeted(k):
+        pl.semaphore_wait(round_sem.at[k], len(near))
 
     own_rows = pl.ds(1 + core * R, R)
 
@@ -135,7 +140,7 @@
 
     weights(WA, w_in, w_out)
 
-    pl.semaphore_wait(barrier, nt - 1 + ntile - 1)
+    pl.semaphore_wait(barrier, 1 + len(near) + len(across))
 
     def send_inputs(first, second):
         remote(first, X.at[:, own_rows], in_send.at[0], in_recv.at[0], mate).start()
@@ -177,8 +182,7 @@
     def _():
         send_inputs(frames, cot)
 
-    for d in range(1, nt):
-        remote(DG.at[tm], DG.at[tm], carry_send.at[0], carry_recv.at[0], on_tm(d)).start()
+    greet(0)
 
     def edge_took(which, field):
         @pl.when(y > 0)
@@ -242,7 +246,6 @@
                     value = value + COEF[i : i + 1] * LS[i - 1, rows, :]
                 LS[i, rows, :] = value
             FIN[rows, :] = encode(last * value)
-            send_finals(row0, count)
 
     def rows_of(ref, k):
         return ref.at[pl.ds(pl.multiple_of(k * W, W), W)]
@@ -259,17 +262,24 @@
 
     took(X.at[:, pl.ds(1, R)], load_sem.at[0])
     widen(X, X3, 1 + core * R, R)
+    greeted(0)
+    greet(1)
     local_scan((core * R + 1, R - 2))
+    greeted(1)
+    greet(2)
     took(X.at[:, pl.ds(1, R)], in_recv.at[0])
     widen(X, X3, 1 + (1 - core) * R, R)
-    if R > 2:
-        local_scan(((1 - core) * (R - 1) + core, R))
-    else:
-        local_scan((1, RC - 2))
+    local_scan(((1 - core) * (R - 1) + core, R) if R > 2 else (1, RC - 2))
+    greeted(2)
+    send_finals(1, RC - 2)
+    for d in range(1, nt):
+        remote(DG.at[tm], DG.at[tm], carry_send.at[0], carry_recv.at[0], on_tm(d)).start()
     edge_took(0, X)
     widen(X, X3, 0, 1)
     widen(X, X3, RC + 1, 1)
     local_scan((0, 1), (RC - 1, 1))
+    send_finals(0, 1)
+    send_finals(RC - 1, 1)
 
     others = pl.ds(0, nt - 1)
     RF[tm] = FIN[pl.ds(pl.multiple_of(tm * W, W), W), :]
@@ -539,6 +549,7 @@
                 dma((2,)), dma((2,)), dma((2,)), dma((3, 2)), dma((3, 2)),
                 dma((1,)), dma((2,)), dma((nt,)), dma((nt,)), dma((nt,)),
                 dma((6,)), dma((12,)), dma((T,)), dma((T,)),
+                pltpu.SemaphoreType.REGULAR((3,)),
             ],
             compiler_params=pltpu.CompilerParams(
                 collective_id=0, has_side_effects=True, vmem_limit_bytes=65_300_000

time: 47.4 us -> 48.3 us (1.019)
  Pallas kernels: 46.6 us -> 47.5 us
    pallas_call x1, Pallas kernels: 45.2 us -> 46.1 us  [step(): pl.pallas_call(functools.partial(chain_kernel, (nt, nx, ny, factor)), out...]
where the time goes in v1:
time: 48.3 us; the launch traced here: 48.1 us
  Pallas kernels  47.5 us (98%)
  between operations  0.64 us (1%)
    pallas_call x1, Pallas kernels, step(): pl.pallas_call(functools.partial(chain_kernel, (nt, nx, ny, factor)), out...  46.1 us
    pallas_call x1, Pallas kernels, step(): pl.pallas_call(store_kernel, out_shape=(jax.ShapeDtypeStruct(frames.shape...  1.4 us

profile of v1, /device:TPU:1, one launch (start us, length us, event | category | flops | bytes accessed | tf_op | source)
XLA Modules:
  0.0 48.1 jit_solution(16040301523216145502)
XLA Ops:
  0.6 46.1 %shard_map.93 = (bf16[4,8,64,128]{3,2,1,0:T(8,128)(2,1)S(1)}, bf16[4,8,64,128]{3,2,1,0:T(8,128)(2,1)S(1)}, bf16[2304,128]{1,0:T(8,128)(2,1)S(1)}) custom-call(bf16[4,8,64,128]{3,2,1,0:T(8,128)(2,1)} %frames.1, bf16[4,8,64,128]{3,2,1,0:T(8,128)(2,1)} %cot.1, bf16[1152,128]{1,0:T(8,128)(2,1)} %bitcast.5, bf16[1152,128]{1,0:T(8,128)(2,1)} %bitcast.6, ...), custom_call_target="tpu_custom_call" | custom-call | tf_op jit(solution)/shard_map/pallas_call | solution.py:533
  46.7 1.4 %shard_map.94 = (bf16[4,8,64,128]{3,2,1,0:T(8,128)(2,1)}, bf16[4,8,64,128]{3,2,1,0:T(8,128)(2,1)}, f32[1152,128]{1,0:T(8,128)}, f32[1152,128]{1,0:T(8,128)}) custom-call(bf16[4,8,64,128]{3,2,1,0:T(8,128)(2,1)S(1)} %get-tuple-element.11.own_out, bf16[4,8,64,128]{3,2,1,0:T(8,128)(2,1)S(1)} %get-tuple-element.12.mate_out, ...), custom_call_target="tpu_custom_call" | custom-call | tf_op jit(solution)/shard_map/pallas_call | solution.py:561

commit v2 on v0

--- a/solution.py
+++ b/solution.py
@@ -27,11 +27,11 @@
 
 def chain_kernel(
     dims,
-    frames, cot, w_in, w_out, skip, log_decay,
+    frames, cot, w_in_hbm, w_out_hbm, skip_hbm, log_decay_hbm,
     own_out, mate_out, sums,
     X, Y, S, X3, Y3, S3, ST,
-    WA, WB, COEF, DG,
-    DR, LS, FIN, RF, EF, INC,
+    w_in, w_out, skip, log_decay, WA, WB, COEF, DG,
+    DR, LS, LST, FIN, RF, EF, INC,
     G, GC, R1, R3, MO,
     load_sem, in_send, in_recv, halo_send, halo_recv,
     carry_send, carry_recv, fin_send, back_send, inc_recv, ar_send, ar_recv, mo_send, mo_recv,
@@ -82,6 +82,14 @@
         )
 
     own_rows = pl.ds(1 + core * R, R)
+    small = [
+        pltpu.make_async_copy(src, dst, load_sem.at[2 + k])
+        for k, (src, dst) in enumerate(
+            (
+                (log_decay_hbm, log_decay), (w_in_hbm, w_in), (w_out_hbm, w_out), (skip_hbm, skip),
+            )
+        )
+    ]
 
     def load(first, second):
         pltpu.make_async_copy(first, X.at[:, own_rows], load_sem.at[0]).start()
@@ -95,16 +103,61 @@
     def _():
         load(cot, frames)
 
-    @pl.when(y == 0)
-    def _():
-        for field in (X, Y, S):
-            field[:, 0] = jnp.zeros((T, W, CH), BF16)
-
-    @pl.when(y == ny - 1)
-    def _():
-        for field in (X, Y, S):
-            field[:, RC + 1] = jnp.zeros((T, W, CH), BF16)
-
+    for copy in small:
+        copy.start()
+
+    pl.semaphore_wait(barrier, nt - 1 + ntile - 1)
+
+    def send_inputs(first, second):
+        remote(first, X.at[:, own_rows], in_send.at[0], in_recv.at[0], mate).start()
+        edge(0)
+        remote(second, Y.at[:, own_rows], in_send.at[1], in_recv.at[1], mate).start()
+        edge(1)
+
+    edge_src = pl.ds(core * (R - 1), 1)
+    edge_dst = pl.ds((1 - core) * (RC + 1), 1)
+    next_y = y + 2 * core - 1
+    has_next = (next_y >= 0) & (next_y < ny)
+    safe_y = lax.min(lax.max(next_y, 0), ny - 1)
+
+    def edge_copies(which):
+        copies = []
+        for c in range(2):
+            src = (frames, cot)[(c == 1) == (which == 1)]
+            dst = (X, Y)[which]
+            copies.append(
+                remote(
+                    src.at[:, edge_src], dst.at[:, edge_dst],
+                    halo_send.at[which, c], halo_recv.at[which, 1 - core],
+                    (tm, safe_y * 2 + c),
+                )
+            )
+        return copies
+
+    def edge(which):
+        @pl.when(has_next)
+        def _():
+            for copy in edge_copies(which):
+                copy.start()
+
+    @pl.when(forward)
+    def _():
+        send_inputs(cot, frames)
+
+    @pl.when(core == 0)
+    def _():
+        send_inputs(frames, cot)
+
+    def edge_took(which, field):
+        @pl.when(y > 0)
+        def _():
+            took(field.at[:, pl.ds(0, 1)], halo_recv.at[which, 0])
+
+        @pl.when(y < ny - 1)
+        def _():
+            took(field.at[:, pl.ds(RC + 1, 1)], halo_recv.at[which, 1])
+
+    small[0].wait()
     dec = jnp.exp(log_decay[...])
     whole = dec[0:1]
     for t in range(1, T):
@@ -133,61 +186,22 @@
             for k in range(9):
                 dst[k * CH : (k + 1) * CH, :] = turned[(8 - k) * CH : (9 - k) * CH, :].T
 
+    for copy in small[1:]:
+        copy.wait()
     weights(WA, w_in, w_out)
-
-    pl.semaphore_wait(barrier, nt - 1 + ntile - 1)
-
-    def send_inputs(first, second):
-        remote(first, X.at[:, own_rows], in_send.at[0], in_recv.at[0], mate).start()
-        edge(0)
-        remote(second, Y.at[:, own_rows], in_send.at[1], in_recv.at[1], mate).start()
-        edge(1)
-
-    edge_src = pl.ds(core * (R - 1), 1)
-    edge_dst = pl.ds((1 - core) * (RC + 1), 1)
-    next_y = y + 2 * core - 1
-    has_next = (next_y >= 0) & (next_y < ny)
-    safe_y = lax.min(lax.max(next_y, 0), ny - 1)
-
-    def edge_copies(which):
-        copies = []
-        for c in range(2):
-            src = (frames, cot)[(c == 1) == (which == 1)]
-            dst = (X, Y)[which]
-            copies.append(
-                remote(
-                    src.at[:, edge_src], dst.at[:, edge_dst],
-                    halo_send.at[which, c], halo_recv.at[which, 1 - core],
-                    (tm, safe_y * 2 + c),
-                )
-            )
-        return copies
-
-    def edge(which):
-        @pl.when(has_next)
-        def _():
-            for copy in edge_copies(which):
-                copy.start()
-
-    @pl.when(forward)
-    def _():
-        send_inputs(cot, frames)
-
-    @pl.when(core == 0)
-    def _():
-        send_inputs(frames, cot)
 
     for d in range(1, nt):
         remote(DG.at[tm], DG.at[tm], carry_send.at[0], carry_recv.at[0], on_tm(d)).start()
 
-    def edge_took(which, field):
-        @pl.when(y > 0)
-        def _():
-            took(field.at[:, pl.ds(0, 1)], halo_recv.at[which, 0])
-
-        @pl.when(y < ny - 1)
-        def _():
-            took(field.at[:, pl.ds(RC + 1, 1)], halo_recv.at[which, 1])
+    @pl.when(y == 0)
+    def _():
+        for field in (X, Y, S):
+            field[:, 0] = jnp.zeros((T, W, CH), BF16)
+
+    @pl.when(y == ny - 1)
+    def _():
+        for field in (X, Y, S):
+            field[:, RC + 1] = jnp.zeros((T, W, CH), BF16)
 
     col = lax.broadcasted_iota(jnp.int32, (1, W, CH), 1)
 
@@ -279,6 +293,9 @@
     took(Y.at[:, pl.ds(1, R)], in_recv.at[1])
     edge_took(1, Y)
     widen(Y, Y3, 0, RC + 2)
+    for i in range(T):
+        LST[i] = LS[i].T
+    turned = COEF[...].T
 
     took(DG.at[others], carry_recv.at[0])
     took(RF.at[others], carry_recv.at[1])
@@ -295,25 +312,19 @@
             carry = DG[k, 0:1, :] * carry + decode(RF[k])
     INC[pl.ds(pl.multiple_of(tm * W, W), W), :] = EF[tm]
 
-    def finish(row0, count):
-        for k in range(row0, row0 + count):
-
-            @pl.when(tm != k)
-            def _():
-                took(rows_of(INC, k), inc_recv.at[k])
-
-        rows = slice(row0 * W, (row0 + count) * W)
-        incoming = decode(INC[rows, :])
-        for i in range(T):
-            value = (
-                COEF[2 * T + i : 2 * T + i + 1] * LS[i, rows, :]
-                + COEF[3 * T + i : 3 * T + i + 1] * incoming
-            )
-            S[frame_of(i), 1 + row0 : 1 + row0 + count] = value.astype(BF16).reshape(count, W, CH)
-
-    finish(1, RC - 2)
-    finish(0, 1)
-    finish(RC - 1, 1)
+    for k in range(nt):
+
+        @pl.when(tm != k)
+        def _():
+            took(rows_of(INC, k), inc_recv.at[k])
+
+    incoming_turned = decode(INC[...].T)
+    for i in range(T):
+        value = (
+            turned[:, 2 * T + i : 2 * T + i + 1] * LST[i]
+            + turned[:, 3 * T + i : 3 * T + i + 1] * incoming_turned
+        )
+        ST[frame_of(i)] = value.astype(BF16)
 
     up = remote(
         S.at[:, pl.ds(1, 1)], S.at[:, pl.ds(RC + 1, 1)], halo_send.at[2, 0], halo_recv.at[2, 1],
@@ -324,14 +335,6 @@
         (tm, lax.min(y + 1, ny - 1) * 2 + core),
     )
 
-    @pl.when(y > 0)
-    def _():
-        up.start()
-
-    @pl.when(y < ny - 1)
-    def _():
-        down.start()
-
     orders = (("x", "y", "z"), ("y", "z", "x"), ("z", "x", "y"))
     steps = [(da, db) for da in range(n) for db in range(n) if da or db]
     steps.sort(key=lambda s: -sum(min(d, n - d) for d in s))
@@ -346,8 +349,6 @@
             at[axis] = lax.rem(at[axis] + d, n)
         return (at["z"] * nx + at["x"], at["y"] * 2 + core)
 
-    for t in range(T):
-        ST[t] = S[t, 1 : RC + 1].reshape(pos, CH).T
     for g in range(3):
         first = core * (2 - g) + (1 - core) * g
         total = jnp.zeros((CH, 3 * CH), F32)
@@ -384,6 +385,19 @@
             value = conv(S3, t, start, R, WB) + direct
             stage[t] = value.astype(BF16).reshape(R, W, CH)
         remote(MO.at[t], mate_out.at[t], mo_send.at[t], mo_recv.at[t], mate).start()
+
+    incoming = decode(INC[...])
+    for i in range(T):
+        value = COEF[2 * T + i : 2 * T + i + 1] * LS[i] + COEF[3 * T + i : 3 * T + i + 1] * incoming
+        S[frame_of(i), 1 : RC + 1] = value.astype(BF16).reshape(RC, W, CH)
+
+    @pl.when(y > 0)
+    def _():
+        up.start()
+
+    @pl.when(y < ny - 1)
+    def _():
+        down.start()
 
     widen(S, S3, 1, RC)
 
@@ -527,16 +541,17 @@
                 vm(frames.shape, BF16),
                 vm((2 * half, CH), BF16),
             ),
-            in_specs=[hbm, hbm, vmem, vmem, vmem, vmem],
+            in_specs=[hbm] * 6,
             out_specs=[vmem] * 3,
             scratch_shapes=[
                 field, field, field, field3, field3, field3, vm((T, CH, pos), BF16),
+                vm((half, CH), BF16), vm((half, CH), BF16), vm((1, CH), F32), vm((T, CH), F32),
                 vm((half, CH), BF16), vm((half, CH), BF16), vm((4 * T, CH), F32), vm((nt, 8, CH), F32),
-                vm((T, pos, CH), F32), vm((T, pos, CH), F32), vm((pos, CH), BF16),
+                vm((T, pos, CH), F32), vm((T, pos, CH), F32), vm((T, CH, pos), F32), vm((pos, CH), BF16),
                 vm((nt, W, CH), BF16), vm((nt, W, CH), BF16), vm((pos, CH), BF16),
                 vm((half, CH), F32), vm((half, CH), BF16),
                 vm((3, n * n - 1, chunk, CH), BF16), vm((3, n, chunk, CH), F32), vm(frames.shape, BF16),
-                dma((2,)), dma((2,)), dma((2,)), dma((3, 2)), dma((3, 2)),
+                dma((6,)), dma((2,)), dma((2,)), dma((3, 2)), dma((3, 2)),
                 dma((1,)), dma((2,)), dma((nt,)), dma((nt,)), dma((nt,)),
                 dma((6,)), dma((12,)), dma((T,)), dma((T,)),
             ],

time: 47.4 us -> 48.5 us (1.023)
  Pallas kernels: 46.6 us -> 47.6 us
    pallas_call x1, Pallas kernels: 45.2 us -> 46.2 us  [step(): pl.pallas_call(functools.partial(chain_kernel, (nt, nx, ny, factor)), out...]
where the time goes in v2:
time: 48.5 us; the launch traced here: 48.4 us
  Pallas kernels  47.6 us (98%)
  between operations  0.8 us (2%)
    pallas_call x1, Pallas kernels, step(): pl.pallas_call(functools.partial(chain_kernel, (nt, nx, ny, factor)), out...  46.2 us
    pallas_call x1, Pallas kernels, step(): pl.pallas_call(store_kernel, out_shape=(jax.ShapeDtypeStruct(frames.shape...  1.4 us

profile of v2, /device:TPU:1, one launch (start us, length us, event | category | flops | bytes accessed | tf_op | source)
XLA Modules:
  0.0 48.4 jit_solution(16028956022052230730)
XLA Ops:
  0.6 46.2 %shard_map.93 = (bf16[4,8,64,128]{3,2,1,0:T(8,128)(2,1)S(1)}, bf16[4,8,64,128]{3,2,1,0:T(8,128)(2,1)S(1)}, bf16[2304,128]{1,0:T(8,128)(2,1)S(1)}) custom-call(bf16[4,8,64,128]{3,2,1,0:T(8,128)(2,1)} %frames.1, bf16[4,8,64,128]{3,2,1,0:T(8,128)(2,1)} %cot.1, bf16[1152,128]{1,0:T(8,128)(2,1)} %bitcast.5, bf16[1152,128]{1,0:T(8,128)(2,1)} %bitcast.6, ...), custom_call_target="tpu_custom_call" | custom-call | tf_op jit(solution)/shard_map/pallas_call | solution.py:537
  46.8 1.4 %shard_map.94 = (bf16[4,8,64,128]{3,2,1,0:T(8,128)(2,1)}, bf16[4,8,64,128]{3,2,1,0:T(8,128)(2,1)}, f32[1152,128]{1,0:T(8,128)}, f32[1152,128]{1,0:T(8,128)}) custom-call(bf16[4,8,64,128]{3,2,1,0:T(8,128)(2,1)S(1)} %get-tuple-element.11.own_out, bf16[4,8,64,128]{3,2,1,0:T(8,128)(2,1)S(1)} %get-tuple-element.12.mate_out, ...), custom_call_target="tpu_custom_call" | custom-call | tf_op jit(solution)/shard_map/pallas_call | solution.py:565

commit v3 on v2

--- a/solution.py
+++ b/solution.py
@@ -31,7 +31,7 @@
     own_out, mate_out, sums,
     X, Y, S, X3, Y3, S3, ST,
     w_in, w_out, skip, log_decay, WA, WB, COEF, DG,
-    DR, LS, LST, FIN, RF, EF, INC,
+    DR, LS, FIN, RF, EF, INC,
     G, GC, R1, R3, MO,
     load_sem, in_send, in_recv, halo_send, halo_recv,
     carry_send, carry_recv, fin_send, back_send, inc_recv, ar_send, ar_recv, mo_send, mo_recv,
@@ -293,9 +293,6 @@
     took(Y.at[:, pl.ds(1, R)], in_recv.at[1])
     edge_took(1, Y)
     widen(Y, Y3, 0, RC + 2)
-    for i in range(T):
-        LST[i] = LS[i].T
-    turned = COEF[...].T
 
     took(DG.at[others], carry_recv.at[0])
     took(RF.at[others], carry_recv.at[1])
@@ -312,19 +309,25 @@
             carry = DG[k, 0:1, :] * carry + decode(RF[k])
     INC[pl.ds(pl.multiple_of(tm * W, W), W), :] = EF[tm]
 
-    for k in range(nt):
-
-        @pl.when(tm != k)
-        def _():
-            took(rows_of(INC, k), inc_recv.at[k])
-
-    incoming_turned = decode(INC[...].T)
-    for i in range(T):
-        value = (
-            turned[:, 2 * T + i : 2 * T + i + 1] * LST[i]
-            + turned[:, 3 * T + i : 3 * T + i + 1] * incoming_turned
-        )
-        ST[frame_of(i)] = value.astype(BF16)
+    def finish(row0, count):
+        for k in range(row0, row0 + count):
+
+            @pl.when(tm != k)
+            def _():
+                took(rows_of(INC, k), inc_recv.at[k])
+
+        rows = slice(row0 * W, (row0 + count) * W)
+        incoming = decode(INC[rows, :])
+        for i in range(T):
+            value = (
+                COEF[2 * T + i : 2 * T + i + 1] * LS[i, rows, :]
+                + COEF[3 * T + i : 3 * T + i + 1] * incoming
+            )
+            S[frame_of(i), 1 + row0 : 1 + row0 + count] = value.astype(BF16).reshape(count, W, CH)
+
+    finish(1, RC - 2)
+    finish(0, 1)
+    finish(RC - 1, 1)
 
     up = remote(
         S.at[:, pl.ds(1, 1)], S.at[:, pl.ds(RC + 1, 1)], halo_send.at[2, 0], halo_recv.at[2, 1],
@@ -335,6 +338,14 @@
         (tm, lax.min(y + 1, ny - 1) * 2 + core),
     )
 
+    @pl.when(y > 0)
+    def _():
+        up.start()
+
+    @pl.when(y < ny - 1)
+    def _():
+        down.start()
+
     orders = (("x", "y", "z"), ("y", "z", "x"), ("z", "x", "y"))
     steps = [(da, db) for da in range(n) for db in range(n) if da or db]
     steps.sort(key=lambda s: -sum(min(d, n - d) for d in s))
@@ -349,6 +360,8 @@
             at[axis] = lax.rem(at[axis] + d, n)
         return (at["z"] * nx + at["x"], at["y"] * 2 + core)
 
+    for t in range(T):
+        ST[t] = S[t, 1 : RC + 1].reshape(pos, CH).T
     for g in range(3):
         first = core * (2 - g) + (1 - core) * g
         total = jnp.zeros((CH, 3 * CH), F32)
@@ -385,19 +398,6 @@
             value = conv(S3, t, start, R, WB) + direct
             stage[t] = value.astype(BF16).reshape(R, W, CH)
         remote(MO.at[t], mate_out.at[t], mo_send.at[t], mo_recv.at[t], mate).start()
-
-    incoming = decode(INC[...])
-    for i in range(T):
-        value = COEF[2 * T + i : 2 * T + i + 1] * LS[i] + COEF[3 * T + i : 3 * T + i + 1] * incoming
-        S[frame_of(i), 1 : RC + 1] = value.astype(BF16).reshape(RC, W, CH)
-
-    @pl.when(y > 0)
-    def _():
-        up.start()
-
-    @pl.when(y < ny - 1)
-    def _():
-        down.start()
 
     widen(S, S3, 1, RC)
 
@@ -547,7 +547,7 @@
                 field, field, field, field3, field3, field3, vm((T, CH, pos), BF16),
                 vm((half, CH), BF16), vm((half, CH), BF16), vm((1, CH), F32), vm((T, CH), F32),
                 vm((half, CH), BF16), vm((half, CH), BF16), vm((4 * T, CH), F32), vm((nt, 8, CH), F32),
-                vm((T, pos, CH), F32), vm((T, pos, CH), F32), vm((T, CH, pos), F32), vm((pos, CH), BF16),
+                vm((T, pos, CH), F32), vm((T, pos, CH), F32), vm((pos, CH), BF16),
                 vm((nt, W, CH), BF16), vm((nt, W, CH), BF16), vm((pos, CH), BF16),
                 vm((half, CH), F32), vm((half, CH), BF16),
                 vm((3, n * n - 1, chunk, CH), BF16), vm((3, n, chunk, CH), F32), vm(frames.shape, BF16),

time: 48.5 us -> 46.4 us (0.957)
  Pallas kernels: 47.6 us -> 45.6 us
    pallas_call x1, Pallas kernels: 46.2 us -> 44.2 us  [step(): pl.pallas_call(functools.partial(chain_kernel, (nt, nx, ny, factor)), out...]
where the time goes in v3:
time: 46.4 us; the launch traced here: 46.2 us
  Pallas kernels  45.6 us (98%)
  between operations  0.64 us (1%)
    pallas_call x1, Pallas kernels, step(): pl.pallas_call(functools.partial(chain_kernel, (nt, nx, ny, factor)), out...  44.2 us
    pallas_call x1, Pallas kernels, step(): pl.pallas_call(store_kernel, out_shape=(jax.ShapeDtypeStruct(frames.shape...  1.4 us

profile of v3, /device:TPU:1, one launch (start us, length us, event | category | flops | bytes accessed | tf_op | source)
XLA Modules:
  0.0 46.2 jit_solution(17803737019211892333)
XLA Ops:
  0.6 44.2 %shard_map.93 = (bf16[4,8,64,128]{3,2,1,0:T(8,128)(2,1)S(1)}, bf16[4,8,64,128]{3,2,1,0:T(8,128)(2,1)S(1)}, bf16[2304,128]{1,0:T(8,128)(2,1)S(1)}) custom-call(bf16[4,8,64,128]{3,2,1,0:T(8,128)(2,1)} %frames.1, bf16[4,8,64,128]{3,2,1,0:T(8,128)(2,1)} %cot.1, bf16[1152,128]{1,0:T(8,128)(2,1)} %bitcast.5, bf16[1152,128]{1,0:T(8,128)(2,1)} %bitcast.6, ...), custom_call_target="tpu_custom_call" | custom-call | tf_op jit(solution)/shard_map/pallas_call | solution.py:537
  44.8 1.4 %shard_map.94 = (bf16[4,8,64,128]{3,2,1,0:T(8,128)(2,1)}, bf16[4,8,64,128]{3,2,1,0:T(8,128)(2,1)}, f32[1152,128]{1,0:T(8,128)}, f32[1152,128]{1,0:T(8,128)}) custom-call(bf16[4,8,64,128]{3,2,1,0:T(8,128)(2,1)S(1)} %get-tuple-element.11.own_out, bf16[4,8,64,128]{3,2,1,0:T(8,128)(2,1)S(1)} %get-tuple-element.12.mate_out, ...), custom_call_target="tpu_custom_call" | custom-call | tf_op jit(solution)/shard_map/pallas_call | solution.py:565

commit v4 on v3

--- a/solution.py
+++ b/solution.py
@@ -436,32 +436,30 @@
         rows = pl.ds(pl.multiple_of(base + g * group + place(g, 0, 0) * chunk, chunk), chunk)
         sums[rows, :] = value.astype(BF16)
         for da, db in steps:
+            peer = plane_peer(g, da, db)
             remote(
-                sums.at[rows], sums.at[rows], ar_send.at[2], ar_recv.at[6 + g],
-                plane_peer(g, da, db),
+                sums.at[rows], sums.at[rows], ar_send.at[2], ar_recv.at[6 + g], peer
             ).start()
+            other = (peer[0], peer[1] + 1 - 2 * core)
+            remote(
+                sums.at[rows], sums.at[rows], ar_send.at[3], ar_recv.at[9 + g], other
+            ).start()
+        remote(sums.at[rows], sums.at[rows], ar_send.at[4], ar_recv.at[9 + g], mate).start()
     conv_out(3)
-    to_mate = []
     for g in range(3):
-        rows = pl.ds(pl.multiple_of(base + g * group, group), group)
         took(sums.at[pl.ds(0, group - chunk)], ar_recv.at[6 + g])
-        to_mate.append(
-            remote(sums.at[rows], sums.at[rows], ar_send.at[3 + g], ar_recv.at[9 + g], mate)
-        )
-        to_mate[-1].start()
+        took(sums.at[pl.ds(0, group)], ar_recv.at[9 + g])
 
     for t in range(T):
         took(MO.at[t], mo_recv.at[t])
-    for copy in to_mate:
-        copy.wait_recv()
-
-    for copy in to_mate:
-        copy.wait_send()
+
     for t in range(T):
         took(MO.at[t], mo_send.at[t])
     took(R1, ar_send.at[0])
     took(R3.at[:, pl.ds(0, n - 1)], ar_send.at[1])
     took(sums.at[pl.ds(0, half - 3 * chunk)], ar_send.at[2])
+    took(sums.at[pl.ds(0, half - 3 * chunk)], ar_send.at[3])
+    took(sums.at[pl.ds(0, 3 * chunk)], ar_send.at[4])
     took(DG.at[others], carry_send.at[0])
     for k in range(nt):
 

time: 46.4 us -> 45.6 us (0.983)
  Pallas kernels: 45.6 us -> 44.7 us
    pallas_call x1, Pallas kernels: 44.2 us -> 43.3 us  [step(): pl.pallas_call(functools.partial(chain_kernel, (nt, nx, ny, factor)), out...]
where the time goes in v4:
time: 45.6 us; the launch traced here: 45.5 us
  Pallas kernels  44.7 us (98%)
  between operations  0.8 us (2%)
    pallas_call x1, Pallas kernels, step(): pl.pallas_call(functools.partial(chain_kernel, (nt, nx, ny, factor)), out...  43.3 us
    pallas_call x1, Pallas kernels, step(): pl.pallas_call(store_kernel, out_shape=(jax.ShapeDtypeStruct(frames.shape...  1.4 us

profile of v4, /device:TPU:1, one launch (start us, length us, event | category | flops | bytes accessed | tf_op | source)
XLA Modules:
  0.0 45.5 jit_solution(1627707855370925301)
XLA Ops:
  0.6 43.3 %shard_map.93 = (bf16[4,8,64,128]{3,2,1,0:T(8,128)(2,1)S(1)}, bf16[4,8,64,128]{3,2,1,0:T(8,128)(2,1)S(1)}, bf16[2304,128]{1,0:T(8,128)(2,1)S(1)}) custom-call(bf16[4,8,64,128]{3,2,1,0:T(8,128)(2,1)} %frames.1, bf16[4,8,64,128]{3,2,1,0:T(8,128)(2,1)} %cot.1, bf16[1152,128]{1,0:T(8,128)(2,1)} %bitcast.5, bf16[1152,128]{1,0:T(8,128)(2,1)} %bitcast.6, ...), custom_call_target="tpu_custom_call" | custom-call | tf_op jit(solution)/shard_map/pallas_call | solution.py:535
  44.0 1.4 %shard_map.94 = (bf16[4,8,64,128]{3,2,1,0:T(8,128)(2,1)}, bf16[4,8,64,128]{3,2,1,0:T(8,128)(2,1)}, f32[1152,128]{1,0:T(8,128)}, f32[1152,128]{1,0:T(8,128)}) custom-call(bf16[4,8,64,128]{3,2,1,0:T(8,128)(2,1)S(1)} %get-tuple-element.11.own_out, bf16[4,8,64,128]{3,2,1,0:T(8,128)(2,1)S(1)} %get-tuple-element.12.mate_out, ...), custom_call_target="tpu_custom_call" | custom-call | tf_op jit(solution)/shard_map/pallas_call | solution.py:563

commit v5 on v4

--- a/solution.py
+++ b/solution.py
@@ -261,11 +261,18 @@
     def rows_of(ref, k):
         return ref.at[pl.ds(pl.multiple_of(k * W, W), W)]
 
+    farthest_first = [
+        lax.rem(z + dz, n) * n + lax.rem(x + dx, n)
+        for dz, dx in sorted(
+            ((dz, dx) for dz in range(n) for dx in range(n) if dz or dx),
+            key=lambda s: -sum(min(d, n - d) for d in s),
+        )
+    ]
+
     def send_finals(row0, count):
-        for r in range(count):
-            k = row0 + lax.rem(r + tm, count)
-
-            @pl.when(k != tm)
+        for k in farthest_first:
+
+            @pl.when((k >= row0) & (k < row0 + count))
             def _():
                 remote(
                     rows_of(FIN, k), RF.at[tm], fin_send.at[k], carry_recv.at[1], (k, tile)
@@ -301,12 +308,10 @@
         k = core * i + (1 - core) * (nt - 1 - i)
         EF[k] = encode(carry)
 
-        @pl.when(k != tm)
-        def _():
-            remote(EF.at[k], rows_of(INC, tm), back_send.at[k], inc_recv.at[tm], (k, tile)).start()
-
         if i < nt - 1:
             carry = DG[k, 0:1, :] * carry + decode(RF[k])
+    for k in farthest_first:
+        remote(EF.at[k], rows_of(INC, tm), back_send.at[k], inc_recv.at[tm], (k, tile)).start()
     INC[pl.ds(pl.multiple_of(tm * W, W), W), :] = EF[tm]
 
     def finish(row0, count):

time: 45.6 us -> 45.2 us (level)
  no operation moved by 1% of the time
where the time goes in v5:
time: 45.2 us; the launch traced here: 45.1 us
  Pallas kernels  44.3 us (98%)
  between operations  0.8 us (2%)
    pallas_call x1, Pallas kernels, step(): pl.pallas_call(functools.partial(chain_kernel, (nt, nx, ny, factor)), out...  42.9 us
    pallas_call x1, Pallas kernels, step(): pl.pallas_call(store_kernel, out_shape=(jax.ShapeDtypeStruct(frames.shape...  1.4 us

profile of v5, /device:TPU:1, one launch (start us, length us, event | category | flops | bytes accessed | tf_op | source)
XLA Modules:
  0.0 45.1 jit_solution(5705930412828283148)
XLA Ops:
  0.6 42.9 %shard_map.93 = (bf16[4,8,64,128]{3,2,1,0:T(8,128)(2,1)S(1)}, bf16[4,8,64,128]{3,2,1,0:T(8,128)(2,1)S(1)}, bf16[2304,128]{1,0:T(8,128)(2,1)S(1)}) custom-call(bf16[4,8,64,128]{3,2,1,0:T(8,128)(2,1)} %frames.1, bf16[4,8,64,128]{3,2,1,0:T(8,128)(2,1)} %cot.1, bf16[1152,128]{1,0:T(8,128)(2,1)} %bitcast.5, bf16[1152,128]{1,0:T(8,128)(2,1)} %bitcast.6, ...), custom_call_target="tpu_custom_call" | custom-call | tf_op jit(solution)/shard_map/pallas_call | solution.py:540
  43.6 1.4 %shard_map.94 = (bf16[4,8,64,128]{3,2,1,0:T(8,128)(2,1)}, bf16[4,8,64,128]{3,2,1,0:T(8,128)(2,1)}, f32[1152,128]{1,0:T(8,128)}, f32[1152,128]{1,0:T(8,128)}) custom-call(bf16[4,8,64,128]{3,2,1,0:T(8,128)(2,1)S(1)} %get-tuple-element.11.own_out, bf16[4,8,64,128]{3,2,1,0:T(8,128)(2,1)S(1)} %get-tuple-element.12.mate_out, ...), custom_call_target="tpu_custom_call" | custom-call | tf_op jit(solution)/shard_map/pallas_call | solution.py:568
